TPU v7x, 32 devices: a whole 2x2x4 slice. The times are simulated.
32 devices in a mesh: grp: 2 (over x), dev: 16 (over z, y, core).
Axes of the slice: x: 2, y: 2, z: 4, core: 2. Of those that a mesh axis runs over, the one named last changes fastest.
Arguments:
- query: bfloat16 [64, 64, 128], P(('grp', 'dev')), may hold values from -6 to 6
- key_cache: bfloat16 [64, 512, 8, 128], P(('grp', 'dev')), may hold values from -6 to 6
- value_cache: bfloat16 [64, 512, 8, 128], P(('grp', 'dev')), may hold values from -6 to 6
- lengths: int32 [64], P(('grp', 'dev')), may hold values from 1 to 512, 16384 in all
- out_weight: bfloat16 [8192, 8192], P('dev', 'grp'), may hold values from -0.0625 to 0.0625
- resid: bfloat16 [64, 8192], P('dev', 'grp'), may hold values from -6 to 6
- norm_gain: bfloat16 [8192], P('grp'), may hold values from 0.5 to 1.5
- gate_weight: bfloat16 [8192, 28672], P('grp', 'dev'), may hold values from -0.0625 to 0.0625
- up_weight: bfloat16 [8192, 28672], P('grp', 'dev'), may hold values from -0.0625 to 0.0625
- down_weight: bfloat16 [28672, 8192], P('dev', 'grp'), may hold values from -0.03125 to 0.03125
Outputs:
- layer_out: bfloat16 [64, 8192], P('dev', 'grp')
Inputs may be any that keep to these rules, and one draw needn't show every extreme that they name: `lengths`: some request has exactly 512 live slots.
All inputs are finite; a program needn't handle non-finite values. No bound on the sum of `lengths` on one device may be relied on, other than what follows from the above.
Results may differ from a plain program's by a relative error of at most 0.015.
Values may be sent and summed in bfloat16 or wider, within the bound.
A program may use at most 128 MiB of HBM per device.

v0:
```python
import jax
import jax.numpy as jnp
from jax import lax
from jax.sharding import PartitionSpec as P


def attend(query, key_cache, value_cache, lengths):
    rows, heads, width = query.shape
    kv_heads = key_cache.shape[2]
    group = heads // kv_heads
    grouped = query.reshape(rows, kv_heads, group, width)
    scores = jnp.einsum(
        "rhgd,rlhd->rhgl", grouped, key_cache, preferred_element_type=jnp.float32
    ) * width ** (-0.5)
    places = jnp.arange(key_cache.shape[1], dtype=jnp.int32)
    valid = places[None, :] < lengths[:, None]
    scores = jnp.where(valid[:, None, None, :], scores, -1e30)
    top = jnp.max(scores, axis=-1, keepdims=True)
    weights = jnp.exp(scores - top)
    probs = (weights / jnp.sum(weights, axis=-1, keepdims=True)).astype(jnp.bfloat16)
    mixed = jnp.einsum("rhgl,rlhd->rhgd", probs, value_cache, preferred_element_type=jnp.float32)
    return mixed.reshape(rows, heads * width).astype(jnp.bfloat16)


def per_device(
    query,
    key_cache,
    value_cache,
    lengths,
    out_weight,
    resid,
    norm_gain,
    gate_weight,
    up_weight,
    down_weight,
):
    attn = attend(query, key_cache, value_cache, lengths)
    block_cols = out_weight.shape[0]
    first_col = lax.axis_index("dev") * block_cols
    cols = lax.dynamic_slice_in_dim(
        lax.all_gather(attn, ("grp", "dev"), axis=0, tiled=True), first_col, block_cols, 1
    )
    proj_terms = jnp.dot(cols, out_weight, preferred_element_type=jnp.float32)
    x = resid.astype(jnp.float32) + lax.psum_scatter(
        proj_terms, "dev", scatter_dimension=0, tiled=True
    )
    width_all = x.shape[1] * lax.axis_size("grp")
    sumsq = lax.psum(jnp.sum(x * x, axis=1), "grp")
    normed = (
        x * lax.rsqrt(sumsq / width_all + 1e-05)[:, None] * norm_gain.astype(jnp.float32)
    ).astype(jnp.bfloat16)
    piece = lax.all_gather(normed, "dev", axis=0, tiled=True)
    half_terms = jnp.concatenate(
        [
            jnp.dot(piece, gate_weight, preferred_element_type=jnp.float32),
            jnp.dot(piece, up_weight, preferred_element_type=jnp.float32),
        ],
        axis=1,
    )
    both = lax.psum(half_terms.astype(jnp.bfloat16), "grp").astype(jnp.float32)
    hidden_cols = gate_weight.shape[1]
    gate = both[:, :hidden_cols]
    up = both[:, hidden_cols:]
    hidden = (jax.nn.silu(gate) * up).astype(jnp.bfloat16)
    ffn_rows = lax.psum_scatter(
        jnp.dot(hidden, down_weight, preferred_element_type=jnp.float32),
        "dev",
        scatter_dimension=0,
        tiled=True,
    )
    return (x + ffn_rows).astype(jnp.bfloat16)


def solution(mesh):
    placed = (
        P(("grp", "dev"), None, None),
        P(("grp", "dev"), None, None, None),
        P(("grp", "dev"), None, None, None),
        P(("grp", "dev")),
        P("dev", "grp"),
        P("dev", "grp"),
        P("grp"),
        P("grp", "dev"),
        P("grp", "dev"),
        P("dev", "grp"),
    )
    return jax.shard_map(
        per_device, mesh=mesh, in_specs=placed, out_specs=P("dev", "grp"), check_vma=False
    )
```

profile of v0, /device:TPU:0, one launch (start us, length us, event | category | flops | bytes accessed | tf_op | source)
XLA Modules:
  0.0 347.9 jit_solution(15746743131024164946)
XLA Ops:
  6.5 0.9 iota_compare_fusion
  7.4 0.7 copy-done
  8.1 1.4 fusion.10
  9.6 0.2 fusion.28
  9.8 2.1 fusion.13
  11.9 0.6 reshape.27
  12.7 56.5 %all-gather.4.cloned.1.call-done = bf16[32,2,8192]{2,1,0:T(2,128)(2,1)} async-done(((bf16[1,2,8192]{2,1,0:T(2,128)(2,1)}), bf16[32,2,8192]{2,1,0:T(2,128)(2,1)}) %all-gather.4.cloned.1.call-update) | async-done | bytes 1048592 | tf_op jit(solution)/shard_map/all_gather | solution.py:41
  69.1 1.5 reshape.28
  70.6 4.1 %fusion.22 = f32[64,4096]{1,0:T(8,128)} fusion(bf16[512,4096]{1,0:T(8,128)(2,1)} %param.14, bf16[64,8192]{1,0:T(8,128)(2,1)S(1)} %reshape.28, s32[]{:T(128)S(6)} %select_n.8), kind=kOutput, calls=%fused_computation.24 | convolution fusion | flops 268435456 | bytes 5308420 | tf_op jit(solution)/shard_map/dot_general | solution.py:43
  74.8 0.6 dynamic-slice
  76.0 91.0 %all-reduce.8.cloned.1.call-done = f32[64,4096]{1,0:T(8,128)} async-done(((f32[64,4096]{1,0:T(8,128)}), f32[64,4096]{1,0:T(8,128)}) %all-reduce.8.cloned.1.call-update) | async-done | bytes 1048592
  167.0 1.1 multiply_reduce_fusion
  168.1 4.9 %psum.14 = f32[4]{0:T(128)S(1)} all-reduce(f32[4]{0:T(128)S(1)} %multiply_reduce_fusion), channel_id=1, replica_groups=mesh['grp'=2,'dev'=16] {'grp'}, use_global_device_ids=true, to_apply=%region_4.5 | all-reduce | flops 4 | bytes 32 | tf_op jit(solution)/shard_map/psum | solution.py:48
  173.0 1.0 fusion.24
  174.0 21.1 %all-gather.1 = bf16[16,4,4096]{2,1,0:T(4,128)(2,1)S(1)} all-gather(bf16[1,4,4096]{2,1,0:T(4,128)(2,1)S(1)} %fusion.24), channel_id=1, replica_groups=mesh['grp'=2,'dev'=16] {'dev'}, dimensions={0}, use_global_device_ids=true | all-gather | bytes 557056 | tf_op jit(solution)/shard_map/all_gather | solution.py:52
  195.1 0.1 reshape.30
  195.2 7.8 %convolution_convert_fusion = bf16[64,1792]{1,0:T(8,128)(2,1)S(1)} fusion(bf16[64,4096]{1,0:T(8,128)(2,1)S(1)} %reshape.30, bf16[4096,1792]{1,0:T(8,128)(2,1)} %param.18), kind=kOutput, calls=%fused_computation.1 | convolution fusion | flops 939638784 | bytes 15433728 | tf_op jit(solution)/shard_map/dot_general | solution.py:56
  203.0 7.8 %convolution_convert_fusion.1 = bf16[64,1792]{1,0:T(8,128)(2,1)S(1)} fusion(bf16[64,4096]{1,0:T(8,128)(2,1)S(1)} %reshape.30, bf16[4096,1792]{1,0:T(8,128)(2,1)} %param.17), kind=kOutput, calls=%fused_computation.2 | convolution fusion | flops 939638784 | bytes 15433728 | tf_op jit(solution)/shard_map/dot_general | solution.py:55
  210.8 0.8 pad_maximum_fusion
  211.7 24.5 %all-reduce.6.cloned.1.call-done = bf16[64,3584]{1,0:T(8,128)(2,1)} async-done(((bf16[64,3584]{1,0:T(8,128)(2,1)}), bf16[64,3584]{1,0:T(8,128)(2,1)}) %all-reduce.6.cloned.1.call-update) | async-done | bytes 458768 | tf_op jit(solution)/shard_map/psum | solution.py:60
  236.3 1.1 convert_element_type.34
  237.3 8.8 %fusion.17 = f32[64,4096]{1,0:T(8,128)} fusion(bf16[1792,4096]{1,0:T(8,128)(2,1)} %param.19, f32[64,3584]{1,0:T(8,128)S(1)} %convert_element_type.34), kind=kOutput, calls=%fused_computation.16 | convolution fusion | flops 940212224 | bytes 16646144 | tf_op jit(solution)/shard_map/dot_general | solution.py:66
  246.2 93.5 %all-reduce.10.cloned.1.call-done = f32[64,4096]{1,0:T(8,128)} async-done(((f32[64,4096]{1,0:T(8,128)}), f32[64,4096]{1,0:T(8,128)}) %all-reduce.10.cloned.1.call-update) | async-done | bytes 1048592
  339.7 1.6 fusion.21
  (17 shorter events, 0.2 us)
Async XLA Ops:
  6.5 1.6 copy-start
  6.5 62.6 %all-gather.4.cloned.1.call-start = ((), (), s32[]{:S(2)}) async-start(), calls=%async_computation.1 | async-start | bytes 1081344 | tf_op jit(solution)/shard_map/all_gather | solution.py:41
  12.6 154.4 %all-reduce.8.cloned.1.call-start = ((), (), s32[]{:S(2)}) async-start(), calls=%async_computation.2 | async-start | bytes 2097152
  12.6 62.1 %copy-start.3 = (u32[32]{0:T(128)S(1)}, u32[32]{0:T(128)}, u32[]{:S(2)}) copy-start(u32[32]{0:T(128)} %constant.33) | copy-start | bytes 388
  12.6 154.4 %copy-start.1 = (bf16[4,4096]{1,0:T(4,128)(2,1)S(1)}, bf16[4,4096]{1,0:T(4,128)(2,1)}, u32[]{:S(2)}) copy-start(bf16[4,4096]{1,0:T(4,128)(2,1)} %param.15) | copy-start | bytes 98308
  12.6 155.4 %copy-start.2 = (bf16[4096]{0:T(1024)(128)(2,1)S(1)}, bf16[4096]{0:T(1024)(128)(2,1)}, u32[]{:S(2)}) copy-start(bf16[4096]{0:T(1024)(128)(2,1)} %param.16) | copy-start | bytes 24580
  74.7 161.6 %all-reduce.6.cloned.1.call-start = ((), (), s32[]{:S(2)}) async-start(), calls=%async_computation | async-start | bytes 917504 | tf_op jit(solution)/shard_map/psum | solution.py:60
  211.7 128.1 %all-reduce.10.cloned.1.call-start = ((), (), s32[]{:S(2)}) async-start(), calls=%async_computation.3 | async-start | bytes 2097152
Sparse Core Ops, SparseCore 0:
  12.7 56.4 all-gather.3
  74.8 92.1 all-reduce.7
  211.8 24.4 all-reduce.5
  246.3 93.3 all-reduce.9
where the time goes:
time: 348 us
  waiting for transfers between devices  266 us (76%)
  matrix products  32.1 us (9%)
  blocking collectives  26 us (7%)
  between operations  13.9 us (4%)
  other arithmetic  6.65 us (2%)
  local copies, waits for them, and re-layouts  3.56 us (1%)
    unnamed x6, waiting for transfers between devices  185 us
    all_gather x1, waiting for transfers between devices, per_device(): lax.all_gather(attn, ('grp', 'dev'), axis=0, tiled=True)  56.5 us
    psum x1, waiting for transfers between devices, per_device(): both = lax.psum(half_terms.astype(jnp.bfloat16), 'grp').astype(jnp.float32)  24.5 us
    all_gather x1, blocking collectives, per_device(): piece = lax.all_gather(normed, 'dev', axis=0, tiled=True)  21.1 us
    dot_general x1, matrix products, per_device(): jnp.dot(hidden, down_weight, preferred_element_type=jnp.float32)  8.84 us
    dot_general x1, matrix products, per_device(): jnp.dot(piece, up_weight, preferred_element_type=jnp.float32)  7.81 us
    dot_general x1, matrix products, per_device(): jnp.dot(piece, gate_weight, preferred_element_type=jnp.float32)  7.81 us
  transfers between devices with their start and end apart: 4, of which 4 were waited for; matrix products, arithmetic and copies ran while one was open for 0% of the time, Pallas kernels for 0%

commit v1 on v0

--- a/solution.py
+++ b/solution.py
@@ -2,6 +2,12 @@
 import jax.numpy as jnp
 from jax import lax
 from jax.sharding import PartitionSpec as P
+
+
+def in_order(parts, dim):
+    shape = list(parts.shape[1:])
+    shape[dim] *= parts.shape[0]
+    return jnp.moveaxis(parts, 0, dim).reshape(shape)
 
 
 def attend(query, key_cache, value_cache, lengths):
@@ -49,7 +55,19 @@
     normed = (
         x * lax.rsqrt(sumsq / width_all + 1e-05)[:, None] * norm_gain.astype(jnp.float32)
     ).astype(jnp.bfloat16)
-    piece = lax.all_gather(normed, "dev", axis=0, tiled=True)
+    peers = lax.axis_size("dev")
+    pairs = [(i, (i + 1) % peers) for i in range(peers)]
+    back = [(b, a) for a, b in pairs]
+    lower, upper = ([], [])
+    for turn in range(peers - 1):
+        if turn % 2 == 0:
+            lower.append(lax.ppermute(lower[-1] if lower else normed, "dev", pairs))
+        else:
+            upper.append(lax.ppermute(upper[-1] if upper else normed, "dev", back))
+    parts = jnp.stack([*lower[::-1], normed, *upper])
+    shift = lax.axis_index("dev") - len(lower)
+    parts = parts[(jnp.arange(peers) - shift) % peers]
+    piece = in_order(parts, 0)
     half_terms = jnp.concatenate(
         [
             jnp.dot(piece, gate_weight, preferred_element_type=jnp.float32),

time: 348 us -> 381 us (1.095)
  starting transfers between devices: 0.13 us -> 31.3 us
  blocking collectives: 26 us -> 4.94 us
  waiting for transfers between devices: 266 us -> 286 us
    ppermute x0 -> x15, starting transfers between devices: none -> 31.2 us  [the longest x7 31.1 us: per_device(): upper.append(lax.ppermute(upper[-1] if upper else normed, 'dev', back))]
    all_gather x1 -> x0, blocking collectives: 21.1 us -> none  [per_device(): piece = lax.all_gather(normed, 'dev', axis=0, tiled=True)]
    ppermute x0 -> x15, waiting for transfers between devices: none -> 17.1 us  [the longest x8 17 us: per_device(): lower.append(lax.ppermute(lower[-1] if lower else normed, 'dev', pairs))]
  transfers between devices with their start and end apart: 4 -> 19, of which waited for: 4 -> 13; matrix products, arithmetic and copies ran while one was open for 0% -> 0% of each run, Pallas kernels for 0% -> 0%
where the time goes in v1:
time: 381 us; the launch traced here: 380 us
  waiting for transfers between devices  286 us (75%)
  matrix products  32.1 us (8%)
  starting transfers between devices  31.3 us (8%)
  between operations  14 us (4%)
  other arithmetic  6.69 us (2%)
  blocking collectives  4.94 us (1%)
  local copies, waits for them, and re-layouts  4.93 us (1%)
    unnamed x6, waiting for transfers between devices  185 us
    all_gather x1, waiting for transfers between devices, per_device(): lax.all_gather(attn, ('grp', 'dev'), axis=0, tiled=True)  56.6 us
    ppermute x7, starting transfers between devices, per_device(): upper.append(lax.ppermute(upper[-1] if upper else normed, 'dev', back))  31.1 us
    psum x1, waiting for transfers between devices, per_device(): both = lax.psum(half_terms.astype(jnp.bfloat16), 'grp').astype(jnp.float32)  28.1 us
    ppermute x8, waiting for transfers between devices, per_device(): lower.append(lax.ppermute(lower[-1] if lower else normed, 'dev', pairs))  17 us
    dot_general x1, matrix products, per_device(): jnp.dot(hidden, down_weight, preferred_element_type=jnp.float32)  8.85 us
    dot_general x1, matrix products, per_device(): jnp.dot(piece, up_weight, preferred_element_type=jnp.float32)  7.81 us
    dot_general x1, matrix products, per_device(): jnp.dot(piece, gate_weight, preferred_element_type=jnp.float32)  7.8 us
  transfers between devices with their start and end apart: 19, of which 13 were waited for; matrix products, arithmetic and copies ran while one was open for 0% of the time, Pallas kernels for 0%

profile of v1, /device:TPU:0, one launch (start us, length us, event | category | flops | bytes accessed | tf_op | source)
XLA Modules:
  0.0 380.3 jit_solution(3090173944395670997)
XLA Ops:
  9.8 2.1 fusion.13
  12.7 56.6 %all-gather.3.cloned.1.call-done = bf16[32,2,8192]{2,1,0:T(2,128)(2,1)} async-done(((bf16[1,2,8192]{2,1,0:T(2,128)(2,1)}), bf16[32,2,8192]{2,1,0:T(2,128)(2,1)}) %all-gather.3.cloned.1.call-update) | async-done | bytes 1048592 | tf_op jit(solution)/shard_map/all_gather | solution.py:47
  70.7 4.1 %fusion.22 = f32[64,4096]{1,0:T(8,128)} fusion(bf16[512,4096]{1,0:T(8,128)(2,1)} %param.14, bf16[64,8192]{1,0:T(8,128)(2,1)S(1)} %reshape.89, s32[]{:T(128)S(6)} %select_n.32), kind=kOutput, calls=%fused_computation.25 | convolution fusion | flops 268435456 | bytes 5308420 | tf_op jit(solution)/shard_map/dot_general | solution.py:49
  76.1 91.0 %all-reduce.8.cloned.1.call-done = f32[64,4096]{1,0:T(8,128)} async-done(((f32[64,4096]{1,0:T(8,128)}), f32[64,4096]{1,0:T(8,128)}) %all-reduce.8.cloned.1.call-update) | async-done | bytes 1048592
  168.2 4.9 %psum.14 = f32[4]{0:T(128)S(1)} all-reduce(f32[4]{0:T(128)S(1)} %multiply_reduce_fusion), channel_id=1, replica_groups=mesh['grp'=2,'dev'=16] {'grp'}, use_global_device_ids=true, to_apply=%region_4.5 | all-reduce | flops 4 | bytes 32 | tf_op jit(solution)/shard_map/psum | solution.py:54
  174.2 6.0 %collective-permute-done = bf16[4,4096]{1,0:T(4,128)(2,1)S(1)} collective-permute-done((bf16[4,4096]{1,0:T(4,128)(2,1)S(1)}, bf16[4,4096]{1,0:T(4,128)(2,1)S(1)}, u32[]{:S(2)}, u32[]{:S(2)}) %collective-permute-start) | collective-permute-done | bytes 32800 | tf_op jit(solution)/shard_map/ppermute | solution.py:64
  180.3 4.4 %collective-permute-start.8 = (bf16[4,4096]{1,0:T(4,128)(2,1)S(1)}, bf16[4,4096]{1,0:T(4,128)(2,1)S(1)}, u32[]{:S(2)}, u32[]{:S(2)}) collective-permute-start(bf16[4,4096]{1,0:T(4,128)(2,1)S(1)} %multiply_convert_fusion), channel_id=1, source_target_pairs={{1,0},{2,1},{3,2},{4,3},{5,4},{6,5},{7,6},{8,7},{9,8},{10,9},{11,1... | collective-permute-start | bytes 98312 | tf_op jit(solution)/shard_map/ppermute | solution.py:66
  184.7 1.6 collective-permute-done.1
  186.3 4.4 %collective-permute-start.9 = (bf16[4,4096]{1,0:T(4,128)(2,1)S(1)}, bf16[4,4096]{1,0:T(4,128)(2,1)S(1)}, u32[]{:S(2)}, u32[]{:S(2)}) collective-permute-start(bf16[4,4096]{1,0:T(4,128)(2,1)S(1)} %collective-permute-done.8), channel_id=1, source_target_pairs={{1,0},{2,1},{3,2},{4,3},{5,4},{6,5},{7,6},{8,7},{9,8},{10,9},{11,1... | collective-permute-start | bytes 98312 | tf_op jit(solution)/shard_map/ppermute | solution.py:66
  190.8 1.6 collective-permute-done.2
  192.3 4.4 %collective-permute-start.10 = (bf16[4,4096]{1,0:T(4,128)(2,1)S(1)}, bf16[4,4096]{1,0:T(4,128)(2,1)S(1)}, u32[]{:S(2)}, u32[]{:S(2)}) collective-permute-start(bf16[4,4096]{1,0:T(4,128)(2,1)S(1)} %collective-permute-done.9), channel_id=1, source_target_pairs={{1,0},{2,1},{3,2},{4,3},{5,4},{6,5},{7,6},{8,7},{9,8},{10,9},{11,1... | collective-permute-start | bytes 98312 | tf_op jit(solution)/shard_map/ppermute | solution.py:66
  196.8 1.6 collective-permute-done.3
  198.4 4.4 %collective-permute-start.11 = (bf16[4,4096]{1,0:T(4,128)(2,1)S(1)}, bf16[4,4096]{1,0:T(4,128)(2,1)S(1)}, u32[]{:S(2)}, u32[]{:S(2)}) collective-permute-start(bf16[4,4096]{1,0:T(4,128)(2,1)S(1)} %collective-permute-done.10), channel_id=1, source_target_pairs={{1,0},{2,1},{3,2},{4,3},{5,4},{6,5},{7,6},{8,7},{9,8},{10,9},{11,1... | collective-permute-start | bytes 98312 | tf_op jit(solution)/shard_map/ppermute | solution.py:66
  202.8 1.6 collective-permute-done.4
  204.4 4.4 %collective-permute-start.12 = (bf16[4,4096]{1,0:T(4,128)(2,1)S(1)}, bf16[4,4096]{1,0:T(4,128)(2,1)S(1)}, u32[]{:S(2)}, u32[]{:S(2)}) collective-permute-start(bf16[4,4096]{1,0:T(4,128)(2,1)S(1)} %collective-permute-done.11), channel_id=1, source_target_pairs={{1,0},{2,1},{3,2},{4,3},{5,4},{6,5},{7,6},{8,7},{9,8},{10,9},{11,1... | collective-permute-start | bytes 98312 | tf_op jit(solution)/shard_map/ppermute | solution.py:66
  208.9 1.6 collective-permute-done.5
  210.5 4.5 %collective-permute-start.13 = (bf16[4,4096]{1,0:T(4,128)(2,1)S(1)}, bf16[4,4096]{1,0:T(4,128)(2,1)S(1)}, u32[]{:S(2)}, u32[]{:S(2)}) collective-permute-start(bf16[4,4096]{1,0:T(4,128)(2,1)S(1)} %collective-permute-done.12), channel_id=1, source_target_pairs={{1,0},{2,1},{3,2},{4,3},{5,4},{6,5},{7,6},{8,7},{9,8},{10,9},{11,1... | collective-permute-start | bytes 98312 | tf_op jit(solution)/shard_map/ppermute | solution.py:66
  216.6 4.4 %collective-permute-start.14 = (bf16[4,4096]{1,0:T(4,128)(2,1)S(1)}, bf16[4,4096]{1,0:T(4,128)(2,1)S(1)}, u32[]{:S(2)}, u32[]{:S(2)}) collective-permute-start(bf16[4,4096]{1,0:T(4,128)(2,1)S(1)} %collective-permute-done.13), channel_id=1, source_target_pairs={{1,0},{2,1},{3,2},{4,3},{5,4},{6,5},{7,6},{8,7},{9,8},{10,9},{11,1... | collective-permute-start | bytes 98312 | tf_op jit(solution)/shard_map/ppermute | solution.py:66
  224.1 7.8 %convolution_convert_fusion = bf16[64,1792]{1,0:T(8,128)(2,1)S(1)} fusion(bf16[64,4096]{1,0:T(8,128)(2,1)S(1)} %reshape.79, bf16[4096,1792]{1,0:T(8,128)(2,1)} %param.18), kind=kOutput, calls=%fused_computation.2 | convolution fusion | flops 939638784 | bytes 15433728 | tf_op jit(solution)/shard_map/dot_general | solution.py:74
  231.9 7.8 %convolution_convert_fusion.1 = bf16[64,1792]{1,0:T(8,128)(2,1)S(1)} fusion(bf16[64,4096]{1,0:T(8,128)(2,1)S(1)} %reshape.79, bf16[4096,1792]{1,0:T(8,128)(2,1)} %param.17), kind=kOutput, calls=%fused_computation.3 | convolution fusion | flops 939638784 | bytes 15433728 | tf_op jit(solution)/shard_map/dot_general | solution.py:73
  240.6 28.1 %all-reduce.6.cloned.1.call-done = bf16[64,3584]{1,0:T(8,128)(2,1)} async-done(((bf16[64,3584]{1,0:T(8,128)(2,1)}), bf16[64,3584]{1,0:T(8,128)(2,1)}) %all-reduce.6.cloned.1.call-update) | async-done | bytes 458768 | tf_op jit(solution)/shard_map/psum | solution.py:78
  269.8 8.8 %fusion.17 = f32[64,4096]{1,0:T(8,128)} fusion(bf16[1792,4096]{1,0:T(8,128)(2,1)} %param.19, f32[64,3584]{1,0:T(8,128)S(1)} %convert_element_type.34), kind=kOutput, calls=%fused_computation.17 | convolution fusion | flops 940212224 | bytes 16646144 | tf_op jit(solution)/shard_map/dot_general | solution.py:84
  278.6 93.5 %all-reduce.10.cloned.1.call-done = f32[64,4096]{1,0:T(8,128)} async-done(((f32[64,4096]{1,0:T(8,128)}), f32[64,4096]{1,0:T(8,128)}) %all-reduce.10.cloned.1.call-update) | async-done | bytes 1048592
  372.1 1.6 fusion.21
  (65 shorter events, 14.8 us)
Async XLA Ops:
  6.5 1.6 copy-start
  6.5 62.7 %all-gather.3.cloned.1.call-start = ((), (), s32[]{:S(2)}) async-start(), calls=%async_computation.1 | async-start | bytes 1081344 | tf_op jit(solution)/shard_map/all_gather | solution.py:47
  12.6 154.6 %all-reduce.8.cloned.1.call-start = ((), (), s32[]{:S(2)}) async-start(), calls=%async_computation.2 | async-start | bytes 2097152
  12.6 62.2 %copy-start.3 = (u32[32]{0:T(128)S(1)}, u32[32]{0:T(128)}, u32[]{:S(2)}) copy-start(u32[32]{0:T(128)} %constant.52) | copy-start | bytes 388
  12.6 154.5 %copy-start.1 = (bf16[4,4096]{1,0:T(4,128)(2,1)S(1)}, bf16[4,4096]{1,0:T(4,128)(2,1)}, u32[]{:S(2)}) copy-start(bf16[4,4096]{1,0:T(4,128)(2,1)} %param.15) | copy-start | bytes 98308
  12.6 155.6 %copy-start.2 = (bf16[4096]{0:T(1024)(128)(2,1)S(1)}, bf16[4096]{0:T(1024)(128)(2,1)}, u32[]{:S(2)}) copy-start(bf16[4096]{0:T(1024)(128)(2,1)} %param.16) | copy-start | bytes 24580
  74.8 193.9 %all-reduce.6.cloned.1.call-start = ((), (), s32[]{:S(2)}) async-start(), calls=%async_computation | async-start | bytes 917504 | tf_op jit(solution)/shard_map/psum | solution.py:78
  174.2 6.1 %collective-permute-start = (bf16[4,4096]{1,0:T(4,128)(2,1)S(1)}, bf16[4,4096]{1,0:T(4,128)(2,1)S(1)}, u32[]{:S(2)}, u32[]{:S(2)}) collective-permute-start(bf16[4,4096]{1,0:T(4,128)(2,1)S(1)} %multiply_convert_fusion), channel_id=1, source_target_pairs={{0,1},{1,2},{2,3},{3,4},{4,5},{5,6},{6,7},{7,8},{8,9},{9,10},{10,1... | collective-permute-start | bytes 98312 | tf_op jit(solution)/shard_map/ppermute | solution.py:64
  180.3 6.0 %collective-permute-start.1 = (bf16[4,4096]{1,0:T(4,128)(2,1)S(1)}, bf16[4,4096]{1,0:T(4,128)(2,1)S(1)}, u32[]{:S(2)}, u32[]{:S(2)}) collective-permute-start(bf16[4,4096]{1,0:T(4,128)(2,1)S(1)} %collective-permute-done), channel_id=1, source_target_pairs={{0,1},{1,2},{2,3},{3,4},{4,5},{5,6},{6,7},{7,8},{8,9},{9,10},{10,1... | collective-permute-start | bytes 98312 | tf_op jit(solution)/shard_map/ppermute | solution.py:64
  180.3 6.0 %collective-permute-start.8 = (bf16[4,4096]{1,0:T(4,128)(2,1)S(1)}, bf16[4,4096]{1,0:T(4,128)(2,1)S(1)}, u32[]{:S(2)}, u32[]{:S(2)}) collective-permute-start(bf16[4,4096]{1,0:T(4,128)(2,1)S(1)} %multiply_convert_fusion), channel_id=1, source_target_pairs={{1,0},{2,1},{3,2},{4,3},{5,4},{6,5},{7,6},{8,7},{9,8},{10,9},{11,1... | collective-permute-start | bytes 98312 | tf_op jit(solution)/shard_map/ppermute | solution.py:66
  186.3 6.0 %collective-permute-start.2 = (bf16[4,4096]{1,0:T(4,128)(2,1)S(1)}, bf16[4,4096]{1,0:T(4,128)(2,1)S(1)}, u32[]{:S(2)}, u32[]{:S(2)}) collective-permute-start(bf16[4,4096]{1,0:T(4,128)(2,1)S(1)} %collective-permute-done.1), channel_id=1, source_target_pairs={{0,1},{1,2},{2,3},{3,4},{4,5},{5,6},{6,7},{7,8},{8,9},{9,10},{10,1... | collective-permute-start | bytes 98312 | tf_op jit(solution)/shard_map/ppermute | solution.py:64
  186.3 6.0 %collective-permute-start.9 = (bf16[4,4096]{1,0:T(4,128)(2,1)S(1)}, bf16[4,4096]{1,0:T(4,128)(2,1)S(1)}, u32[]{:S(2)}, u32[]{:S(2)}) collective-permute-start(bf16[4,4096]{1,0:T(4,128)(2,1)S(1)} %collective-permute-done.8), channel_id=1, source_target_pairs={{1,0},{2,1},{3,2},{4,3},{5,4},{6,5},{7,6},{8,7},{9,8},{10,9},{11,1... | collective-permute-start | bytes 98312 | tf_op jit(solution)/shard_map/ppermute | solution.py:66
  192.3 6.0 %collective-permute-start.3 = (bf16[4,4096]{1,0:T(4,128)(2,1)S(1)}, bf16[4,4096]{1,0:T(4,128)(2,1)S(1)}, u32[]{:S(2)}, u32[]{:S(2)}) collective-permute-start(bf16[4,4096]{1,0:T(4,128)(2,1)S(1)} %collective-permute-done.2), channel_id=1, source_target_pairs={{0,1},{1,2},{2,3},{3,4},{4,5},{5,6},{6,7},{7,8},{8,9},{9,10},{10,1... | collective-permute-start | bytes 98312 | tf_op jit(solution)/shard_map/ppermute | solution.py:64
  192.3 6.0 %collective-permute-start.10 = (bf16[4,4096]{1,0:T(4,128)(2,1)S(1)}, bf16[4,4096]{1,0:T(4,128)(2,1)S(1)}, u32[]{:S(2)}, u32[]{:S(2)}) collective-permute-start(bf16[4,4096]{1,0:T(4,128)(2,1)S(1)} %collective-permute-done.9), channel_id=1, source_target_pairs={{1,0},{2,1},{3,2},{4,3},{5,4},{6,5},{7,6},{8,7},{9,8},{10,9},{11,1... | collective-permute-start | bytes 98312 | tf_op jit(solution)/shard_map/ppermute | solution.py:66
  198.4 6.0 %collective-permute-start.4 = (bf16[4,4096]{1,0:T(4,128)(2,1)S(1)}, bf16[4,4096]{1,0:T(4,128)(2,1)S(1)}, u32[]{:S(2)}, u32[]{:S(2)}) collective-permute-start(bf16[4,4096]{1,0:T(4,128)(2,1)S(1)} %collective-permute-done.3), channel_id=1, source_target_pairs={{0,1},{1,2},{2,3},{3,4},{4,5},{5,6},{6,7},{7,8},{8,9},{9,10},{10,1... | collective-permute-start | bytes 98312 | tf_op jit(solution)/shard_map/ppermute | solution.py:64
  198.4 6.0 %collective-permute-start.11 = (bf16[4,4096]{1,0:T(4,128)(2,1)S(1)}, bf16[4,4096]{1,0:T(4,128)(2,1)S(1)}, u32[]{:S(2)}, u32[]{:S(2)}) collective-permute-start(bf16[4,4096]{1,0:T(4,128)(2,1)S(1)} %collective-permute-done.10), channel_id=1, source_target_pairs={{1,0},{2,1},{3,2},{4,3},{5,4},{6,5},{7,6},{8,7},{9,8},{10,9},{11,1... | collective-permute-start | bytes 98312 | tf_op jit(solution)/shard_map/ppermute | solution.py:66
  204.4 6.0 %collective-permute-start.5 = (bf16[4,4096]{1,0:T(4,128)(2,1)S(1)}, bf16[4,4096]{1,0:T(4,128)(2,1)S(1)}, u32[]{:S(2)}, u32[]{:S(2)}) collective-permute-start(bf16[4,4096]{1,0:T(4,128)(2,1)S(1)} %collective-permute-done.4), channel_id=1, source_target_pairs={{0,1},{1,2},{2,3},{3,4},{4,5},{5,6},{6,7},{7,8},{8,9},{9,10},{10,1... | collective-permute-start | bytes 98312 | tf_op jit(solution)/shard_map/ppermute | solution.py:64
  204.4 6.0 %collective-permute-start.12 = (bf16[4,4096]{1,0:T(4,128)(2,1)S(1)}, bf16[4,4096]{1,0:T(4,128)(2,1)S(1)}, u32[]{:S(2)}, u32[]{:S(2)}) collective-permute-start(bf16[4,4096]{1,0:T(4,128)(2,1)S(1)} %collective-permute-done.11), channel_id=1, source_target_pairs={{1,0},{2,1},{3,2},{4,3},{5,4},{6,5},{7,6},{8,7},{9,8},{10,9},{11,1... | collective-permute-start | bytes 98312 | tf_op jit(solution)/shard_map/ppermute | solution.py:66
  210.5 6.0 %collective-permute-start.6 = (bf16[4,4096]{1,0:T(4,128)(2,1)S(1)}, bf16[4,4096]{1,0:T(4,128)(2,1)S(1)}, u32[]{:S(2)}, u32[]{:S(2)}) collective-permute-start(bf16[4,4096]{1,0:T(4,128)(2,1)S(1)} %collective-permute-done.5), channel_id=1, source_target_pairs={{0,1},{1,2},{2,3},{3,4},{4,5},{5,6},{6,7},{7,8},{8,9},{9,10},{10,1... | collective-permute-start | bytes 98312 | tf_op jit(solution)/shard_map/ppermute | solution.py:64
  210.5 6.1 %collective-permute-start.13 = (bf16[4,4096]{1,0:T(4,128)(2,1)S(1)}, bf16[4,4096]{1,0:T(4,128)(2,1)S(1)}, u32[]{:S(2)}, u32[]{:S(2)}) collective-permute-start(bf16[4,4096]{1,0:T(4,128)(2,1)S(1)} %collective-permute-done.12), channel_id=1, source_target_pairs={{1,0},{2,1},{3,2},{4,3},{5,4},{6,5},{7,6},{8,7},{9,8},{10,9},{11,1... | collective-permute-start | bytes 98312 | tf_op jit(solution)/shard_map/ppermute | solution.py:66
  216.5 6.0 %collective-permute-start.7 = (bf16[4,4096]{1,0:T(4,128)(2,1)S(1)}, bf16[4,4096]{1,0:T(4,128)(2,1)S(1)}, u32[]{:S(2)}, u32[]{:S(2)}) collective-permute-start(bf16[4,4096]{1,0:T(4,128)(2,1)S(1)} %collective-permute-done.6), channel_id=1, source_target_pairs={{0,1},{1,2},{2,3},{3,4},{4,5},{5,6},{6,7},{7,8},{8,9},{9,10},{10,1... | collective-permute-start | bytes 98312 | tf_op jit(solution)/shard_map/ppermute | solution.py:64
  216.6 6.4 %collective-permute-start.14 = (bf16[4,4096]{1,0:T(4,128)(2,1)S(1)}, bf16[4,4096]{1,0:T(4,128)(2,1)S(1)}, u32[]{:S(2)}, u32[]{:S(2)}) collective-permute-start(bf16[4,4096]{1,0:T(4,128)(2,1)S(1)} %collective-permute-done.13), channel_id=1, source_target_pairs={{1,0},{2,1},{3,2},{4,3},{5,4},{6,5},{7,6},{8,7},{9,8},{10,9},{11,1... | collective-permute-start | bytes 98312 | tf_op jit(solution)/shard_map/ppermute | solution.py:66
  240.6 131.6 %all-reduce.10.cloned.1.call-start = ((), (), s32[]{:S(2)}) async-start(), calls=%async_computation.3 | async-start | bytes 2097152
Sparse Core Ops, SparseCore 0:
  12.7 56.5 all-gather.2
  74.9 92.1 all-reduce.7
  240.7 27.9 all-reduce.5
  278.8 93.3 all-reduce.9
